TPU v7x, 32 devices: a whole 2x2x4 slice. The times are simulated.
32 devices in a mesh: cuts: 1, state: 32 (over z, y, x, core).
Axes of the slice: x: 2, y: 2, z: 4, core: 2. Of those that a mesh axis runs over, the one named last changes fastest.
Arguments:
- initial_states: bfloat16 [256, 32, 48, 128], P(('cuts', 'state')), may hold values from -36 to 36
- potential: float32 [32, 48, 128], replicated, may hold values from -1 to 0
- bounds: int32 [2], P('cuts'), may hold values from -32 to 159, as said below
Outputs:
- orthonormal: float32 [256, 196608], P('cuts', 'state')
Inputs may be any that keep to these rules, and one draw needn't show every extreme that they name: `bounds`: the first entry lies in -32 to -17, inside the spectrum of H, and the second in 136 to 159, above it; the anchor -1.125 lies below the spectrum.
All inputs are finite; a program needn't handle non-finite values.
Results may differ from a plain program's by a relative error of at most 0.0003.
Values sent between devices are 32-bit elements; how exact they have to be, the bound alone decides.
No kernel may reach another device: no remote copies, remote signals or barrier semaphores. Data moves between devices by JAX's collectives and lax.ppermute only.
A program may use at most 192 MiB of HBM per device.

v0:
```python
import math
import jax
import jax.numpy as jnp
from jax import lax
from jax.sharding import PartitionSpec as P

DEGREE = 16
STENCIL_NEAR = 4.0 / 3.0
STENCIL_FAR = -1.0 / 12.0
STENCIL_SELF = -5.0 / 2.0
ANCHOR_VALUE = -1.125


def laplace_periodic(values, axis_dim):
    near_sum = jnp.roll(values, 1, axis_dim) + jnp.roll(values, -1, axis_dim)
    far_sum = jnp.roll(values, 2, axis_dim) + jnp.roll(values, -2, axis_dim)
    return STENCIL_NEAR * near_sum + STENCIL_FAR * far_sum


def laplace_walled(values):
    extent = values.shape[1]
    padded = jnp.pad(values, ((0, 0), (2, 2), (0, 0), (0, 0)))
    near_sum = padded[:, 1 : extent + 1] + padded[:, 3 : extent + 3]
    far_sum = padded[:, 0:extent] + padded[:, 4 : extent + 4]
    return STENCIL_NEAR * near_sum + STENCIL_FAR * far_sum


def apply_hamiltonian(values, potential):
    laplace = 3.0 * STENCIL_SELF * values + laplace_walled(values)
    laplace = laplace + laplace_periodic(values, 2) + laplace_periodic(values, 3)
    return -0.5 * laplace + potential[None] * values


def filter_states(states, potential, bounds):
    low_end = bounds[0].astype(jnp.float32) / 64.0
    high_end = bounds[1].astype(jnp.float32) / 16.0
    half_width = (high_end - low_end) / 2.0
    centre = (high_end + low_end) / 2.0
    sigma_now = half_width / (ANCHOR_VALUE - centre)
    tau_value = 2.0 / sigma_now
    current = (apply_hamiltonian(states, potential) - centre * states) * (sigma_now / half_width)

    def degree_step(degree, carried):
        previous, current, sigma_now = carried
        sigma_next = 1.0 / (tau_value - sigma_now)
        latest = (apply_hamiltonian(current, potential) - centre * current) * (
            2.0 * sigma_next / half_width
        )
        latest = latest - sigma_now * sigma_next * previous
        return (current, latest, sigma_next)

    carried = lax.fori_loop(1, DEGREE, degree_step, (states, current, sigma_now))
    return carried[1]


def outer_product(left, right):
    return lax.dot_general(
        left,
        right,
        (((1,), (1,)), ((), ())),
        precision=lax.Precision.HIGHEST,
        preferred_element_type=jnp.float32,
    )


def per_device(initial_states, potential, bounds):
    filtered = filter_states(initial_states.astype(jnp.float32), potential, bounds)
    points = filtered.shape[1] * filtered.shape[2] * filtered.shape[3]
    flat = filtered.reshape(filtered.shape[0], points)
    row_block = lax.all_to_all(flat, "state", split_axis=1, concat_axis=0, tiled=True)
    gram_local = outer_product(row_block, row_block)
    gram_total = lax.psum(gram_local, "state")
    factor = jnp.linalg.cholesky(gram_total)
    solved = lax.linalg.triangular_solve(factor, row_block, left_side=True, lower=True)
    return solved * math.sqrt(points)


def solution(mesh):
    return jax.shard_map(
        per_device,
        mesh=mesh,
        in_specs=(P(("cuts", "state"), None, None, None), P(), P("cuts")),
        out_specs=P("cuts", "state"),
        check_vma=False,
    )
```

profile of v0, /device:TPU:0, one launch (start us, length us, event | category | flops | bytes accessed | tf_op | source)
XLA Modules:
  0.0 1869.4 jit_solution(1136967705735163389)
XLA Ops:
  9.2 8.4 fusion.55
  50.8 37.2 %fusion.28 = f32[8,32,48,128]{3,2,1,0:T(8,128)} fusion(f32[8,32,48,128]{3,2,1,0:T(8,128)} %convert_element_type.16, f32[8,32,47,128]{3,2,1,0:T(8,128)} %get-tuple-element.170, f32[8,32,1,128]{3,2,1,0:T(1,128)S(1)} %get-tuple-element.172, f32[8,32,1,128]{3,2,1,0:T(1,128)S(1)} %get-tuple-element.171, f32[8,32,47,128]{3,2,1,0:T(8,128)} %get-tuple-element.169, ...), kind=kLoop, calls=%fused_computation.43 | loop fusion | flops 51904512 | bytes 63701000 | tf_op jit(solution)/shard_map/mul | solution.py:41
  87.9 1411.8 %while.17 = (s32[]{:T(128)}, f32[8,32,48,128]{3,2,1,0:T(8,128)}, f32[8,32,48,128]{3,2,1,0:T(8,128)}, f32[]{:T(128)}, f32[32,48,128]{2,1,0:T(8,128)S(1)}, /*index...) while((s32[]{:T(128)}, f32[8,32,48,128]{3,2,1,0:T(8,128)}, ...), condition=%wide.region_1.2_spmd, body=%wide.region_0.1_spmd.sunk | while | flops 55050248 | bytes 243007824 | solution.py:52
  88.0 10.6 fusion.78
  104.3 6.7 fusion.82
  132.7 39.8 %fusion.86 = f32[8,32,48,128]{3,2,1,0:T(8,128)} fusion(f32[8,32,48,128]{3,2,1,0:T(8,128)} %get-tuple-element.306, f32[8,32,47,128]{3,2,1,0:T(8,128)} %get-tuple-element.271, f32[8,32,1,128]{3,2,1,0:T(1,128)} %get-tuple-element.272, f32[8,32,1,128]{3,2,1,0:T(1,128)S(1)} %get-tuple-element.273, f32[8,32,47,128]{3,2,1,0:T(8,128)} %get-tuple-element.274, ...), kind=kLoop, calls=%fused_computation.14.clone.1 | loop fusion | flops 55050240 | bytes 69992464 | tf_op jit(solution)/shard_map/while/body/eval_jaxpr/sub | solution.py:49
  181.4 10.6 fusion.78
  197.7 6.7 fusion.82
  226.1 39.8 %fusion.86 = f32[8,32,48,128]{3,2,1,0:T(8,128)} fusion(f32[8,32,48,128]{3,2,1,0:T(8,128)} %get-tuple-element.306, f32[8,32,47,128]{3,2,1,0:T(8,128)} %get-tuple-element.271, f32[8,32,1,128]{3,2,1,0:T(1,128)} %get-tuple-element.272, f32[8,32,1,128]{3,2,1,0:T(1,128)S(1)} %get-tuple-element.273, f32[8,32,47,128]{3,2,1,0:T(8,128)} %get-tuple-element.274, ...), kind=kLoop, calls=%fused_computation.14.clone.1 | loop fusion | flops 55050240 | bytes 69992464 | tf_op jit(solution)/shard_map/while/body/eval_jaxpr/sub | solution.py:49
  274.7 10.6 fusion.78
  291.1 6.7 fusion.82
  319.5 39.8 %fusion.86 = f32[8,32,48,128]{3,2,1,0:T(8,128)} fusion(f32[8,32,48,128]{3,2,1,0:T(8,128)} %get-tuple-element.306, f32[8,32,47,128]{3,2,1,0:T(8,128)} %get-tuple-element.271, f32[8,32,1,128]{3,2,1,0:T(1,128)} %get-tuple-element.272, f32[8,32,1,128]{3,2,1,0:T(1,128)S(1)} %get-tuple-element.273, f32[8,32,47,128]{3,2,1,0:T(8,128)} %get-tuple-element.274, ...), kind=kLoop, calls=%fused_computation.14.clone.1 | loop fusion | flops 55050240 | bytes 69992464 | tf_op jit(solution)/shard_map/while/body/eval_jaxpr/sub | solution.py:49
  368.1 10.6 fusion.78
  412.8 39.8 %fusion.86 = f32[8,32,48,128]{3,2,1,0:T(8,128)} fusion(f32[8,32,48,128]{3,2,1,0:T(8,128)} %get-tuple-element.306, f32[8,32,47,128]{3,2,1,0:T(8,128)} %get-tuple-element.271, f32[8,32,1,128]{3,2,1,0:T(1,128)} %get-tuple-element.272, f32[8,32,1,128]{3,2,1,0:T(1,128)S(1)} %get-tuple-element.273, f32[8,32,47,128]{3,2,1,0:T(8,128)} %get-tuple-element.274, ...), kind=kLoop, calls=%fused_computation.14.clone.1 | loop fusion | flops 55050240 | bytes 69992464 | tf_op jit(solution)/shard_map/while/body/eval_jaxpr/sub | solution.py:49
  461.5 10.6 fusion.78
  477.8 6.7 fusion.82
  506.2 39.8 %fusion.86 = f32[8,32,48,128]{3,2,1,0:T(8,128)} fusion(f32[8,32,48,128]{3,2,1,0:T(8,128)} %get-tuple-element.306, f32[8,32,47,128]{3,2,1,0:T(8,128)} %get-tuple-element.271, f32[8,32,1,128]{3,2,1,0:T(1,128)} %get-tuple-element.272, f32[8,32,1,128]{3,2,1,0:T(1,128)S(1)} %get-tuple-element.273, f32[8,32,47,128]{3,2,1,0:T(8,128)} %get-tuple-element.274, ...), kind=kLoop, calls=%fused_computation.14.clone.1 | loop fusion | flops 55050240 | bytes 69992464 | tf_op jit(solution)/shard_map/while/body/eval_jaxpr/sub | solution.py:49
  554.9 10.6 fusion.78
  599.6 39.8 %fusion.86 = f32[8,32,48,128]{3,2,1,0:T(8,128)} fusion(f32[8,32,48,128]{3,2,1,0:T(8,128)} %get-tuple-element.306, f32[8,32,47,128]{3,2,1,0:T(8,128)} %get-tuple-element.271, f32[8,32,1,128]{3,2,1,0:T(1,128)} %get-tuple-element.272, f32[8,32,1,128]{3,2,1,0:T(1,128)S(1)} %get-tuple-element.273, f32[8,32,47,128]{3,2,1,0:T(8,128)} %get-tuple-element.274, ...), kind=kLoop, calls=%fused_computation.14.clone.1 | loop fusion | flops 55050240 | bytes 69992464 | tf_op jit(solution)/shard_map/while/body/eval_jaxpr/sub | solution.py:49
  648.3 10.6 fusion.78
  664.6 6.7 fusion.82
  693.0 39.8 %fusion.86 = f32[8,32,48,128]{3,2,1,0:T(8,128)} fusion(f32[8,32,48,128]{3,2,1,0:T(8,128)} %get-tuple-element.306, f32[8,32,47,128]{3,2,1,0:T(8,128)} %get-tuple-element.271, f32[8,32,1,128]{3,2,1,0:T(1,128)} %get-tuple-element.272, f32[8,32,1,128]{3,2,1,0:T(1,128)S(1)} %get-tuple-element.273, f32[8,32,47,128]{3,2,1,0:T(8,128)} %get-tuple-element.274, ...), kind=kLoop, calls=%fused_computation.14.clone.1 | loop fusion | flops 55050240 | bytes 69992464 | tf_op jit(solution)/shard_map/while/body/eval_jaxpr/sub | solution.py:49
  741.7 10.6 fusion.78
  758.0 6.7 fusion.82
  786.4 39.8 %fusion.86 = f32[8,32,48,128]{3,2,1,0:T(8,128)} fusion(f32[8,32,48,128]{3,2,1,0:T(8,128)} %get-tuple-element.306, f32[8,32,47,128]{3,2,1,0:T(8,128)} %get-tuple-element.271, f32[8,32,1,128]{3,2,1,0:T(1,128)} %get-tuple-element.272, f32[8,32,1,128]{3,2,1,0:T(1,128)S(1)} %get-tuple-element.273, f32[8,32,47,128]{3,2,1,0:T(8,128)} %get-tuple-element.274, ...), kind=kLoop, calls=%fused_computation.14.clone.1 | loop fusion | flops 55050240 | bytes 69992464 | tf_op jit(solution)/shard_map/while/body/eval_jaxpr/sub | solution.py:49
  835.0 10.6 fusion.78
  851.4 6.7 fusion.82
  879.8 39.8 %fusion.86 = f32[8,32,48,128]{3,2,1,0:T(8,128)} fusion(f32[8,32,48,128]{3,2,1,0:T(8,128)} %get-tuple-element.306, f32[8,32,47,128]{3,2,1,0:T(8,128)} %get-tuple-element.271, f32[8,32,1,128]{3,2,1,0:T(1,128)} %get-tuple-element.272, f32[8,32,1,128]{3,2,1,0:T(1,128)S(1)} %get-tuple-element.273, f32[8,32,47,128]{3,2,1,0:T(8,128)} %get-tuple-element.274, ...), kind=kLoop, calls=%fused_computation.14.clone.1 | loop fusion | flops 55050240 | bytes 69992464 | tf_op jit(solution)/shard_map/while/body/eval_jaxpr/sub | solution.py:49
  928.4 10.6 fusion.78
  944.7 6.7 fusion.82
  973.1 39.8 %fusion.86 = f32[8,32,48,128]{3,2,1,0:T(8,128)} fusion(f32[8,32,48,128]{3,2,1,0:T(8,128)} %get-tuple-element.306, f32[8,32,47,128]{3,2,1,0:T(8,128)} %get-tuple-element.271, f32[8,32,1,128]{3,2,1,0:T(1,128)} %get-tuple-element.272, f32[8,32,1,128]{3,2,1,0:T(1,128)S(1)} %get-tuple-element.273, f32[8,32,47,128]{3,2,1,0:T(8,128)} %get-tuple-element.274, ...), kind=kLoop, calls=%fused_computation.14.clone.1 | loop fusion | flops 55050240 | bytes 69992464 | tf_op jit(solution)/shard_map/while/body/eval_jaxpr/sub | solution.py:49
  1021.8 10.6 fusion.78
  1066.5 39.8 %fusion.86 = f32[8,32,48,128]{3,2,1,0:T(8,128)} fusion(f32[8,32,48,128]{3,2,1,0:T(8,128)} %get-tuple-element.306, f32[8,32,47,128]{3,2,1,0:T(8,128)} %get-tuple-element.271, f32[8,32,1,128]{3,2,1,0:T(1,128)} %get-tuple-element.272, f32[8,32,1,128]{3,2,1,0:T(1,128)S(1)} %get-tuple-element.273, f32[8,32,47,128]{3,2,1,0:T(8,128)} %get-tuple-element.274, ...), kind=kLoop, calls=%fused_computation.14.clone.1 | loop fusion | flops 55050240 | bytes 69992464 | tf_op jit(solution)/shard_map/while/body/eval_jaxpr/sub | solution.py:49
  1115.2 10.6 fusion.78
  1131.5 6.7 fusion.82
  1159.9 39.8 %fusion.86 = f32[8,32,48,128]{3,2,1,0:T(8,128)} fusion(f32[8,32,48,128]{3,2,1,0:T(8,128)} %get-tuple-element.306, f32[8,32,47,128]{3,2,1,0:T(8,128)} %get-tuple-element.271, f32[8,32,1,128]{3,2,1,0:T(1,128)} %get-tuple-element.272, f32[8,32,1,128]{3,2,1,0:T(1,128)S(1)} %get-tuple-element.273, f32[8,32,47,128]{3,2,1,0:T(8,128)} %get-tuple-element.274, ...), kind=kLoop, calls=%fused_computation.14.clone.1 | loop fusion | flops 55050240 | bytes 69992464 | tf_op jit(solution)/shard_map/while/body/eval_jaxpr/sub | solution.py:49
  1208.6 10.6 fusion.78
  1253.3 39.8 %fusion.86 = f32[8,32,48,128]{3,2,1,0:T(8,128)} fusion(f32[8,32,48,128]{3,2,1,0:T(8,128)} %get-tuple-element.306, f32[8,32,47,128]{3,2,1,0:T(8,128)} %get-tuple-element.271, f32[8,32,1,128]{3,2,1,0:T(1,128)} %get-tuple-element.272, f32[8,32,1,128]{3,2,1,0:T(1,128)S(1)} %get-tuple-element.273, f32[8,32,47,128]{3,2,1,0:T(8,128)} %get-tuple-element.274, ...), kind=kLoop, calls=%fused_computation.14.clone.1 | loop fusion | flops 55050240 | bytes 69992464 | tf_op jit(solution)/shard_map/while/body/eval_jaxpr/sub | solution.py:49
  1302.0 10.6 fusion.78
  1346.7 39.8 %fusion.86 = f32[8,32,48,128]{3,2,1,0:T(8,128)} fusion(f32[8,32,48,128]{3,2,1,0:T(8,128)} %get-tuple-element.306, f32[8,32,47,128]{3,2,1,0:T(8,128)} %get-tuple-element.271, f32[8,32,1,128]{3,2,1,0:T(1,128)} %get-tuple-element.272, f32[8,32,1,128]{3,2,1,0:T(1,128)S(1)} %get-tuple-element.273, f32[8,32,47,128]{3,2,1,0:T(8,128)} %get-tuple-element.274, ...), kind=kLoop, calls=%fused_computation.14.clone.1 | loop fusion | flops 55050240 | bytes 69992464 | tf_op jit(solution)/shard_map/while/body/eval_jaxpr/sub | solution.py:49
  1395.3 10.6 fusion.78
  1440.1 39.8 %fusion.86 = f32[8,32,48,128]{3,2,1,0:T(8,128)} fusion(f32[8,32,48,128]{3,2,1,0:T(8,128)} %get-tuple-element.306, f32[8,32,47,128]{3,2,1,0:T(8,128)} %get-tuple-element.271, f32[8,32,1,128]{3,2,1,0:T(1,128)} %get-tuple-element.272, f32[8,32,1,128]{3,2,1,0:T(1,128)S(1)} %get-tuple-element.273, f32[8,32,47,128]{3,2,1,0:T(8,128)} %get-tuple-element.274, ...), kind=kLoop, calls=%fused_computation.14.clone.1 | loop fusion | flops 55050240 | bytes 69992464 | tf_op jit(solution)/shard_map/while/body/eval_jaxpr/sub | solution.py:49
  1506.2 145.7 %all_to_all.19 = f32[8,32,6144]{2,0,1:T(8,128)S(1)} all-to-all(f32[8,32,6144]{2,0,1:T(8,128)S(1)} %bitcast.52), channel_id=1, replica_groups=mesh['cuts'=1,'state'=32] {'state'}, dimensions={1} | all-to-all | bytes 12582912 | tf_op jit(solution)/shard_map/all_to_all | solution.py:70
  1660.5 125.8 %all-reduce.5.cloned.1.call-done = f32[256,256]{0,1:T(8,128)} async-done(((f32[256,256]{0,1:T(8,128)}), f32[256,256]{0,1:T(8,128)}) %all-reduce.5.cloned.1.call-update) | async-done | bytes 262160 | tf_op jit(solution)/shard_map/psum | solution.py:72
  1788.4 11.7 cholesky.50
  1800.2 9.8 custom-call.14
  1810.5 11.9 cholesky.105
  1828.5 19.7 %custom-call.15 = f32[2,128,128]{1,2,0:T(8,128)S(1)} custom-call(f32[2,128,128]{2,1,0:T(8,128)S(1)} %get-tuple-element.114), custom_call_target="InvertDiagBlocksLowerTriangular" | custom-call | tf_op jit(solution)/shard_map/triangular_solve | solution.py:74
  (306 shorter events, 657.7 us)
Async XLA Ops:
  6.5 1779.8 %all-reduce.5.cloned.1.call-start = ((), (), s32[]{:S(2)}) async-start(), calls=%async_computation.1 | async-start | bytes 524288 | tf_op jit(solution)/shard_map/psum | solution.py:72
  9.2 8.4 copy-start
  88.0 10.6 slice-start
  88.0 10.6 slice-start.1
  172.5 6.1 copy-start.1
  181.4 10.6 slice-start
  181.4 10.6 slice-start.1
  265.8 6.1 copy-start.1
  274.7 10.6 slice-start
  274.7 10.6 slice-start.1
  359.2 6.1 copy-start.1
  368.1 10.6 slice-start
  368.1 10.6 slice-start.1
  452.6 6.1 copy-start.1
  461.5 10.6 slice-start
  461.5 10.6 slice-start.1
  546.0 6.1 copy-start.1
  554.9 10.6 slice-start
  554.9 10.6 slice-start.1
  639.4 6.1 copy-start.1
  648.3 10.6 slice-start
  648.3 10.6 slice-start.1
  732.8 6.1 copy-start.1
  741.7 10.6 slice-start
  741.7 10.6 slice-start.1
  826.1 6.1 copy-start.1
  835.0 10.6 slice-start
  835.0 10.6 slice-start.1
  919.5 6.1 copy-start.1
  928.4 10.6 slice-start
  928.4 10.6 slice-start.1
  1012.9 6.1 copy-start.1
  1021.8 10.6 slice-start
  1021.8 10.6 slice-start.1
  1106.3 6.1 copy-start.1
  1115.2 10.6 slice-start
  1115.2 10.6 slice-start.1
  1199.7 6.1 copy-start.1
  1208.6 10.6 slice-start
  1208.6 10.6 slice-start.1
  1293.1 6.1 copy-start.1
  1301.9 10.6 slice-start
  1301.9 10.6 slice-start.1
  1386.4 6.1 copy-start.1
  1395.3 10.6 slice-start
  1395.3 10.6 slice-start.1
  1479.8 6.1 copy-start.1
  1848.2 4.9 copy-start.3
  (17 other events, 48.2 us)
Sparse Core Ops, SparseCore 0:
  1660.6 125.6 all-reduce.4
where the time goes:
time: 1880 us; the launch traced here: 1870 us
  local copies, waits for them, and re-layouts  856 us (46%)
  other arithmetic  695 us (37%)
  blocking collectives  146 us (8%)
  waiting for transfers between devices  126 us (7%)
    sub x15, other arithmetic, degree_step(): latest = latest - sigma_now * sigma_next * previous  596 us
    slice x64, local copies, waits for them, and re-layouts, laplace_periodic(): near_sum = jnp.roll(values, 1, axis_dim) + jnp.roll(values, -1, axis_dim)  390 us
    slice x64, local copies, waits for them, and re-layouts, laplace_periodic(): far_sum = jnp.roll(values, 2, axis_dim) + jnp.roll(values, -2, axis_dim)  317 us
    all_to_all x1, blocking collectives, per_device(): lax.all_to_all(flat, 'state', split_axis=1, concat_axis=0, tiled=True)  146 us
    while x150, local copies, waits for them, and re-layouts  133 us
    psum x1, waiting for transfers between devices, per_device(): gram_total = lax.psum(gram_local, 'state')  126 us
  transfers between devices with their start and end apart: 1, of which 1 were waited for; matrix products, arithmetic and copies ran while one was open for 0% of the time, Pallas kernels for 0%

commit v1 on v0

--- a/solution.py
+++ b/solution.py
@@ -67,7 +67,10 @@
     filtered = filter_states(initial_states.astype(jnp.float32), potential, bounds)
     points = filtered.shape[1] * filtered.shape[2] * filtered.shape[3]
     flat = filtered.reshape(filtered.shape[0], points)
-    row_block = lax.all_to_all(flat, "state", split_axis=1, concat_axis=0, tiled=True)
+    row_block = jnp.concatenate(
+        lax.all_to_all(jnp.stack(jnp.split(flat, lax.axis_size("state"), axis=1)), "state", 0, 0),
+        axis=0,
+    )
     gram_local = outer_product(row_block, row_block)
     gram_total = lax.psum(gram_local, "state")
     factor = jnp.linalg.cholesky(gram_total)

time: 1880 us -> 1880 us (level)
    while x151 -> x150, local copies, waits for them, and re-layouts: 140 us -> 133 us
where the time goes in v1:
time: 1880 us; the launch traced here: 1870 us
  local copies, waits for them, and re-layouts  860 us (46%)
  other arithmetic  695 us (37%)
  blocking collectives  146 us (8%)
  waiting for transfers between devices  126 us (7%)
    sub x15, other arithmetic, degree_step(): latest = latest - sigma_now * sigma_next * previous  596 us
    slice x64, local copies, waits for them, and re-layouts, laplace_periodic(): near_sum = jnp.roll(values, 1, axis_dim) + jnp.roll(values, -1, axis_dim)  390 us
    slice x64, local copies, waits for them, and re-layouts, laplace_periodic(): far_sum = jnp.roll(values, 2, axis_dim) + jnp.roll(values, -2, axis_dim)  317 us
    all_to_all x1, blocking collectives, per_device(): lax.all_to_all(jnp.stack(jnp.split(flat, lax.axis_size('state'), axis=1))...  146 us
    while x150, local copies, waits for them, and re-layouts  133 us
    psum x1, waiting for transfers between devices, per_device(): gram_total = lax.psum(gram_local, 'state')  126 us
  transfers between devices with their start and end apart: 1, of which 1 were waited for; matrix products, arithmetic and copies ran while one was open for 0% of the time, Pallas kernels for 0%

profile of v1, /device:TPU:0, one launch (start us, length us, event | category | flops | bytes accessed | tf_op | source)
XLA Modules:
  0.0 1873.3 jit_solution(16462598495090936513)
XLA Ops:
  9.2 8.4 fusion.87
  50.8 37.2 %fusion.28 = f32[8,32,48,128]{3,2,1,0:T(8,128)} fusion(f32[8,32,48,128]{3,2,1,0:T(8,128)} %convert_element_type.16, f32[8,32,47,128]{3,2,1,0:T(8,128)} %get-tuple-element.170, f32[8,32,1,128]{3,2,1,0:T(1,128)S(1)} %get-tuple-element.172, f32[8,32,1,128]{3,2,1,0:T(1,128)S(1)} %get-tuple-element.171, f32[8,32,47,128]{3,2,1,0:T(8,128)} %get-tuple-element.169, ...), kind=kLoop, calls=%fused_computation.43 | loop fusion | flops 51904512 | bytes 63701000 | tf_op jit(solution)/shard_map/mul | solution.py:41
  87.9 1412.2 %while.17 = (s32[]{:T(128)}, f32[8,32,48,128]{3,2,1,0:T(8,128)}, f32[8,32,48,128]{3,2,1,0:T(8,128)}, f32[]{:T(128)}, f32[32,48,128]{2,1,0:T(8,128)S(1)}, /*index...) while((s32[]{:T(128)}, f32[8,32,48,128]{3,2,1,0:T(8,128)}, ...), condition=%wide.region_1.2_spmd, body=%wide.region_0.1_spmd.sunk | while | flops 55050248 | bytes 243007824 | solution.py:52
  88.0 10.6 fusion.110
  104.3 6.7 fusion.114
  132.7 39.8 %fusion.118 = f32[8,32,48,128]{3,2,1,0:T(8,128)} fusion(f32[8,32,48,128]{3,2,1,0:T(8,128)} %get-tuple-element.306, f32[8,32,47,128]{3,2,1,0:T(8,128)} %get-tuple-element.271, f32[8,32,1,128]{3,2,1,0:T(1,128)} %get-tuple-element.272, f32[8,32,1,128]{3,2,1,0:T(1,128)S(1)} %get-tuple-element.273, f32[8,32,47,128]{3,2,1,0:T(8,128)} %get-tuple-element.274, ...), kind=kLoop, calls=%fused_computation.14.clone.1 | loop fusion | flops 55050240 | bytes 69992464 | tf_op jit(solution)/shard_map/while/body/eval_jaxpr/sub | solution.py:49
  181.4 10.6 fusion.110
  197.7 6.7 fusion.114
  226.1 39.8 %fusion.118 = f32[8,32,48,128]{3,2,1,0:T(8,128)} fusion(f32[8,32,48,128]{3,2,1,0:T(8,128)} %get-tuple-element.306, f32[8,32,47,128]{3,2,1,0:T(8,128)} %get-tuple-element.271, f32[8,32,1,128]{3,2,1,0:T(1,128)} %get-tuple-element.272, f32[8,32,1,128]{3,2,1,0:T(1,128)S(1)} %get-tuple-element.273, f32[8,32,47,128]{3,2,1,0:T(8,128)} %get-tuple-element.274, ...), kind=kLoop, calls=%fused_computation.14.clone.1 | loop fusion | flops 55050240 | bytes 69992464 | tf_op jit(solution)/shard_map/while/body/eval_jaxpr/sub | solution.py:49
  274.7 10.6 fusion.110
  291.1 6.7 fusion.114
  319.5 39.8 %fusion.118 = f32[8,32,48,128]{3,2,1,0:T(8,128)} fusion(f32[8,32,48,128]{3,2,1,0:T(8,128)} %get-tuple-element.306, f32[8,32,47,128]{3,2,1,0:T(8,128)} %get-tuple-element.271, f32[8,32,1,128]{3,2,1,0:T(1,128)} %get-tuple-element.272, f32[8,32,1,128]{3,2,1,0:T(1,128)S(1)} %get-tuple-element.273, f32[8,32,47,128]{3,2,1,0:T(8,128)} %get-tuple-element.274, ...), kind=kLoop, calls=%fused_computation.14.clone.1 | loop fusion | flops 55050240 | bytes 69992464 | tf_op jit(solution)/shard_map/while/body/eval_jaxpr/sub | solution.py:49
  368.1 10.6 fusion.110
  412.8 39.8 %fusion.118 = f32[8,32,48,128]{3,2,1,0:T(8,128)} fusion(f32[8,32,48,128]{3,2,1,0:T(8,128)} %get-tuple-element.306, f32[8,32,47,128]{3,2,1,0:T(8,128)} %get-tuple-element.271, f32[8,32,1,128]{3,2,1,0:T(1,128)} %get-tuple-element.272, f32[8,32,1,128]{3,2,1,0:T(1,128)S(1)} %get-tuple-element.273, f32[8,32,47,128]{3,2,1,0:T(8,128)} %get-tuple-element.274, ...), kind=kLoop, calls=%fused_computation.14.clone.1 | loop fusion | flops 55050240 | bytes 69992464 | tf_op jit(solution)/shard_map/while/body/eval_jaxpr/sub | solution.py:49
  461.5 10.6 fusion.110
  477.8 6.7 fusion.114
  506.2 39.8 %fusion.118 = f32[8,32,48,128]{3,2,1,0:T(8,128)} fusion(f32[8,32,48,128]{3,2,1,0:T(8,128)} %get-tuple-element.306, f32[8,32,47,128]{3,2,1,0:T(8,128)} %get-tuple-element.271, f32[8,32,1,128]{3,2,1,0:T(1,128)} %get-tuple-element.272, f32[8,32,1,128]{3,2,1,0:T(1,128)S(1)} %get-tuple-element.273, f32[8,32,47,128]{3,2,1,0:T(8,128)} %get-tuple-element.274, ...), kind=kLoop, calls=%fused_computation.14.clone.1 | loop fusion | flops 55050240 | bytes 69992464 | tf_op jit(solution)/shard_map/while/body/eval_jaxpr/sub | solution.py:49
  554.9 10.6 fusion.110
  599.6 39.8 %fusion.118 = f32[8,32,48,128]{3,2,1,0:T(8,128)} fusion(f32[8,32,48,128]{3,2,1,0:T(8,128)} %get-tuple-element.306, f32[8,32,47,128]{3,2,1,0:T(8,128)} %get-tuple-element.271, f32[8,32,1,128]{3,2,1,0:T(1,128)} %get-tuple-element.272, f32[8,32,1,128]{3,2,1,0:T(1,128)S(1)} %get-tuple-element.273, f32[8,32,47,128]{3,2,1,0:T(8,128)} %get-tuple-element.274, ...), kind=kLoop, calls=%fused_computation.14.clone.1 | loop fusion | flops 55050240 | bytes 69992464 | tf_op jit(solution)/shard_map/while/body/eval_jaxpr/sub | solution.py:49
  648.3 10.6 fusion.110
  664.6 6.7 fusion.114
  693.0 39.8 %fusion.118 = f32[8,32,48,128]{3,2,1,0:T(8,128)} fusion(f32[8,32,48,128]{3,2,1,0:T(8,128)} %get-tuple-element.306, f32[8,32,47,128]{3,2,1,0:T(8,128)} %get-tuple-element.271, f32[8,32,1,128]{3,2,1,0:T(1,128)} %get-tuple-element.272, f32[8,32,1,128]{3,2,1,0:T(1,128)S(1)} %get-tuple-element.273, f32[8,32,47,128]{3,2,1,0:T(8,128)} %get-tuple-element.274, ...), kind=kLoop, calls=%fused_computation.14.clone.1 | loop fusion | flops 55050240 | bytes 69992464 | tf_op jit(solution)/shard_map/while/body/eval_jaxpr/sub | solution.py:49
  741.7 10.6 fusion.110
  758.0 6.7 fusion.114
  786.4 39.8 %fusion.118 = f32[8,32,48,128]{3,2,1,0:T(8,128)} fusion(f32[8,32,48,128]{3,2,1,0:T(8,128)} %get-tuple-element.306, f32[8,32,47,128]{3,2,1,0:T(8,128)} %get-tuple-element.271, f32[8,32,1,128]{3,2,1,0:T(1,128)} %get-tuple-element.272, f32[8,32,1,128]{3,2,1,0:T(1,128)S(1)} %get-tuple-element.273, f32[8,32,47,128]{3,2,1,0:T(8,128)} %get-tuple-element.274, ...), kind=kLoop, calls=%fused_computation.14.clone.1 | loop fusion | flops 55050240 | bytes 69992464 | tf_op jit(solution)/shard_map/while/body/eval_jaxpr/sub | solution.py:49
  835.0 10.6 fusion.110
  851.4 6.7 fusion.114
  879.8 39.8 %fusion.118 = f32[8,32,48,128]{3,2,1,0:T(8,128)} fusion(f32[8,32,48,128]{3,2,1,0:T(8,128)} %get-tuple-element.306, f32[8,32,47,128]{3,2,1,0:T(8,128)} %get-tuple-element.271, f32[8,32,1,128]{3,2,1,0:T(1,128)} %get-tuple-element.272, f32[8,32,1,128]{3,2,1,0:T(1,128)S(1)} %get-tuple-element.273, f32[8,32,47,128]{3,2,1,0:T(8,128)} %get-tuple-element.274, ...), kind=kLoop, calls=%fused_computation.14.clone.1 | loop fusion | flops 55050240 | bytes 69992464 | tf_op jit(solution)/shard_map/while/body/eval_jaxpr/sub | solution.py:49
  928.4 10.6 fusion.110
  944.7 6.7 fusion.114
  973.1 39.8 %fusion.118 = f32[8,32,48,128]{3,2,1,0:T(8,128)} fusion(f32[8,32,48,128]{3,2,1,0:T(8,128)} %get-tuple-element.306, f32[8,32,47,128]{3,2,1,0:T(8,128)} %get-tuple-element.271, f32[8,32,1,128]{3,2,1,0:T(1,128)} %get-tuple-element.272, f32[8,32,1,128]{3,2,1,0:T(1,128)S(1)} %get-tuple-element.273, f32[8,32,47,128]{3,2,1,0:T(8,128)} %get-tuple-element.274, ...), kind=kLoop, calls=%fused_computation.14.clone.1 | loop fusion | flops 55050240 | bytes 69992464 | tf_op jit(solution)/shard_map/while/body/eval_jaxpr/sub | solution.py:49
  1021.8 10.6 fusion.110
  1066.5 39.8 %fusion.118 = f32[8,32,48,128]{3,2,1,0:T(8,128)} fusion(f32[8,32,48,128]{3,2,1,0:T(8,128)} %get-tuple-element.306, f32[8,32,47,128]{3,2,1,0:T(8,128)} %get-tuple-element.271, f32[8,32,1,128]{3,2,1,0:T(1,128)} %get-tuple-element.272, f32[8,32,1,128]{3,2,1,0:T(1,128)S(1)} %get-tuple-element.273, f32[8,32,47,128]{3,2,1,0:T(8,128)} %get-tuple-element.274, ...), kind=kLoop, calls=%fused_computation.14.clone.1 | loop fusion | flops 55050240 | bytes 69992464 | tf_op jit(solution)/shard_map/while/body/eval_jaxpr/sub | solution.py:49
  1115.2 10.6 fusion.110
  1159.9 39.8 %fusion.118 = f32[8,32,48,128]{3,2,1,0:T(8,128)} fusion(f32[8,32,48,128]{3,2,1,0:T(8,128)} %get-tuple-element.306, f32[8,32,47,128]{3,2,1,0:T(8,128)} %get-tuple-element.271, f32[8,32,1,128]{3,2,1,0:T(1,128)} %get-tuple-element.272, f32[8,32,1,128]{3,2,1,0:T(1,128)S(1)} %get-tuple-element.273, f32[8,32,47,128]{3,2,1,0:T(8,128)} %get-tuple-element.274, ...), kind=kLoop, calls=%fused_computation.14.clone.1 | loop fusion | flops 55050240 | bytes 69992464 | tf_op jit(solution)/shard_map/while/body/eval_jaxpr/sub | solution.py:49
  1208.6 10.6 fusion.110
  1253.3 39.8 %fusion.118 = f32[8,32,48,128]{3,2,1,0:T(8,128)} fusion(f32[8,32,48,128]{3,2,1,0:T(8,128)} %get-tuple-element.306, f32[8,32,47,128]{3,2,1,0:T(8,128)} %get-tuple-element.271, f32[8,32,1,128]{3,2,1,0:T(1,128)} %get-tuple-element.272, f32[8,32,1,128]{3,2,1,0:T(1,128)S(1)} %get-tuple-element.273, f32[8,32,47,128]{3,2,1,0:T(8,128)} %get-tuple-element.274, ...), kind=kLoop, calls=%fused_computation.14.clone.1 | loop fusion | flops 55050240 | bytes 69992464 | tf_op jit(solution)/shard_map/while/body/eval_jaxpr/sub | solution.py:49
  1302.0 10.6 fusion.110
  1346.7 39.8 %fusion.118 = f32[8,32,48,128]{3,2,1,0:T(8,128)} fusion(f32[8,32,48,128]{3,2,1,0:T(8,128)} %get-tuple-element.306, f32[8,32,47,128]{3,2,1,0:T(8,128)} %get-tuple-element.271, f32[8,32,1,128]{3,2,1,0:T(1,128)} %get-tuple-element.272, f32[8,32,1,128]{3,2,1,0:T(1,128)S(1)} %get-tuple-element.273, f32[8,32,47,128]{3,2,1,0:T(8,128)} %get-tuple-element.274, ...), kind=kLoop, calls=%fused_computation.14.clone.1 | loop fusion | flops 55050240 | bytes 69992464 | tf_op jit(solution)/shard_map/while/body/eval_jaxpr/sub | solution.py:49
  1395.3 10.6 fusion.110
  1440.1 39.8 %fusion.118 = f32[8,32,48,128]{3,2,1,0:T(8,128)} fusion(f32[8,32,48,128]{3,2,1,0:T(8,128)} %get-tuple-element.306, f32[8,32,47,128]{3,2,1,0:T(8,128)} %get-tuple-element.271, f32[8,32,1,128]{3,2,1,0:T(1,128)} %get-tuple-element.272, f32[8,32,1,128]{3,2,1,0:T(1,128)S(1)} %get-tuple-element.273, f32[8,32,47,128]{3,2,1,0:T(8,128)} %get-tuple-element.274, ...), kind=kLoop, calls=%fused_computation.14.clone.1 | loop fusion | flops 55050240 | bytes 69992464 | tf_op jit(solution)/shard_map/while/body/eval_jaxpr/sub | solution.py:49
  1500.2 9.2 copy.9
  1510.2 145.7 %all_to_all.5 = f32[32,8,6144]{2,1,0:T(8,128)S(1)} all-to-all(f32[32,8,6144]{2,1,0:T(8,128)S(1)} %fusion.41), channel_id=1, replica_groups=mesh['cuts'=1,'state'=32] {'state'}, dimensions={0} | all-to-all | bytes 12582912 | tf_op jit(solution)/shard_map/all_to_all | solution.py:71
  1664.5 125.8 %all-reduce.5.cloned.1.call-done = f32[256,256]{0,1:T(8,128)} async-done(((f32[256,256]{0,1:T(8,128)}), f32[256,256]{0,1:T(8,128)}) %all-reduce.5.cloned.1.call-update) | async-done | bytes 262160 | tf_op jit(solution)/shard_map/psum | solution.py:75
  1792.4 11.7 cholesky.50
  1804.2 9.8 custom-call.14
  1814.5 11.9 cholesky.105
  1832.5 19.7 %custom-call.15 = f32[2,128,128]{1,2,0:T(8,128)S(1)} custom-call(f32[2,128,128]{2,1,0:T(8,128)S(1)} %get-tuple-element.114), custom_call_target="InvertDiagBlocksLowerTriangular" | custom-call | tf_op jit(solution)/shard_map/triangular_solve | solution.py:77
  (338 shorter events, 658.5 us)
Async XLA Ops:
  6.5 1783.8 %all-reduce.5.cloned.1.call-start = ((), (), s32[]{:S(2)}) async-start(), calls=%async_computation.1 | async-start | bytes 524288 | tf_op jit(solution)/shard_map/psum | solution.py:75
  9.2 8.4 copy-start
  88.0 10.6 slice-start
  88.0 10.6 slice-start.1
  172.5 6.1 copy-start.1
  181.4 10.6 slice-start
  181.4 10.6 slice-start.1
  265.8 6.1 copy-start.1
  274.7 10.6 slice-start
  274.7 10.6 slice-start.1
  359.2 6.1 copy-start.1
  368.1 10.6 slice-start
  368.1 10.6 slice-start.1
  452.6 6.1 copy-start.1
  461.5 10.6 slice-start
  461.5 10.6 slice-start.1
  546.0 6.1 copy-start.1
  554.9 10.6 slice-start
  554.9 10.6 slice-start.1
  639.4 6.1 copy-start.1
  648.3 10.6 slice-start
  648.3 10.6 slice-start.1
  732.8 6.1 copy-start.1
  741.7 10.6 slice-start
  741.7 10.6 slice-start.1
  826.1 6.1 copy-start.1
  835.0 10.6 slice-start
  835.0 10.6 slice-start.1
  919.5 6.1 copy-start.1
  928.4 10.6 slice-start
  928.4 10.6 slice-start.1
  1012.9 6.1 copy-start.1
  1021.8 10.6 slice-start
  1021.8 10.6 slice-start.1
  1106.3 6.1 copy-start.1
  1115.2 10.6 slice-start
  1115.2 10.6 slice-start.1
  1199.7 6.1 copy-start.1
  1208.6 10.6 slice-start
  1208.6 10.6 slice-start.1
  1293.1 6.1 copy-start.1
  1301.9 10.6 slice-start
  1301.9 10.6 slice-start.1
  1386.4 6.1 copy-start.1
  1395.3 10.6 slice-start
  1395.3 10.6 slice-start.1
  1479.8 6.1 copy-start.1
  1852.2 4.9 copy-start.3
  (17 other events, 48.2 us)
Sparse Core Ops, SparseCore 0:
  1664.6 125.6 all-reduce.4
